TPU v7x, 32 devices: a whole 2x2x4 slice. The times are simulated.
32 devices in a mesh: row: 4 (over x, core), col: 8 (over z, y).
Axes of the slice: x: 2, y: 2, z: 4, core: 2. Of those that a mesh axis runs over, the one named last changes fastest.
Arguments:
- left_factor: bfloat16 [128, 32, 2048], P('col', None, 'row'), may hold values from -6 to 6
- right_factor: bfloat16 [128, 32, 2048], P('row', None, 'col'), may hold values from -6 to 6
- pair_grad: bfloat16 [2048, 128, 2048], P('row', None, 'col'), may hold values from -6 to 6
- projection: bfloat16 [1024, 128], replicated, may hold values from -0.1875 to 0.1875
Outputs:
- left_grad: float32 [128, 32, 2048], P('col', None, 'row')
- right_grad: float32 [128, 32, 2048], P('row', None, 'col')
All inputs are finite; a program needn't handle non-finite values.
Results may differ from a plain program's by a relative error of at most 0.0029.
Values may be sent and summed in bfloat16 or wider, within the bound.
A program may use at most 576 MiB of HBM per device.

v0:
```python
import functools

import jax
import jax.numpy as jnp
from jax import lax
from jax.experimental import pallas as pl
from jax.experimental.pallas import tpu as pltpu
from jax.sharding import PartitionSpec as P

CHUNKS = 4
BLOCK_ROWS = 16


def contract_block(channels, cols, inverse, proj_ref, grad_ref, left_ref, right_ref, before_ref, out_left_ref, sum_ref, held):
    rows = grad_ref.shape[0]

    @pl.when(pl.program_id(0) == 0)
    def _():
        sum_ref[...] = before_ref[...]

    @pl.loop(0, rows)
    def _(i):
        wide = jnp.dot(proj_ref[...], grad_ref[i], preferred_element_type=jnp.float32)
        wide = wide.astype(jnp.bfloat16)
        at = pl.ds(pl.multiple_of(i * channels, channels), channels)
        for e in range(channels):
            held[at, e * cols : (e + 1) * cols] = wide[e * channels : (e + 1) * channels]

    total = channels * cols
    step = min(1024, total)
    out_left_ref[...] = jnp.zeros_like(out_left_ref)

    @pl.loop(0, total // step)
    def _(n):
        at = pl.ds(pl.multiple_of(n * step, step), step)
        part = held[:, at]
        sum_ref[:, at] += jnp.dot(left_ref[...], part, preferred_element_type=jnp.float32)
        out_left_ref[...] += lax.dot_general(
            right_ref[:, at], part, (((1,), (1,)), ((), ())), preferred_element_type=jnp.float32
        )

    out_left_ref[...] *= inverse


def contract(proj, grad, left, right, before, chunk, chunks):
    tile_rows, width, cols = grad.shape
    sequences = left.shape[0]
    rows = tile_rows // chunks
    channels = left.shape[1] // rows
    block = min(BLOCK_ROWS, rows)
    steps = rows // block
    flops = 2 * rows * cols * channels * channels * (width + 2 * sequences)
    whole = lambda shape: pl.BlockSpec(shape, lambda n: (0, 0))
    return pl.pallas_call(
        functools.partial(contract_block, channels, cols, 1.0 / sequences),
        grid=(steps,),
        in_specs=[
            whole(proj.shape),
            pl.BlockSpec((block, width, cols), lambda n: (chunk * steps + n, 0, 0)),
            pl.BlockSpec((sequences, block * channels), lambda n: (0, n)),
            whole(right.shape),
            whole(before.shape),
        ],
        out_specs=[
            pl.BlockSpec((sequences, block * channels), lambda n: (0, n)),
            whole(before.shape),
        ],
        out_shape=[
            jax.ShapeDtypeStruct((sequences, rows * channels), jnp.float32),
            jax.ShapeDtypeStruct(before.shape, jnp.float32),
        ],
        scratch_shapes=[pltpu.VMEM((block * channels, channels * cols), jnp.bfloat16)],
        input_output_aliases={4: 1},
        compiler_params=pltpu.CompilerParams(
            dimension_semantics=("arbitrary",), vmem_limit_bytes=56 * 1024 * 1024
        ),
        cost_estimate=pl.CostEstimate(
            flops=flops, bytes_accessed=rows * width * cols * 2 + before.size * 8, transcendentals=0
        ),
    )(proj, grad, left, right, before)


def on_device(left_factor, right_factor, pair_grad, projection):
    tile_rows, width, cols = pair_grad.shape
    own, channels, _ = left_factor.shape
    right_own = right_factor.shape[0]
    proj = projection.reshape(channels, channels, width).transpose(1, 0, 2).reshape(channels * channels, width)
    right = lax.all_gather(right_factor.reshape(right_own, channels * cols), "row", axis=0, tiled=True)
    sequences = right.shape[0]
    left_own = jnp.transpose(left_factor, (0, 2, 1)).reshape(own, tile_rows * channels)
    per = tile_rows * channels // CHUNKS
    lefts = [
        lax.all_gather(left_own[:, n * per : (n + 1) * per], "col", axis=0, tiled=True) for n in range(CHUNKS)
    ]
    summed = jnp.zeros((sequences, channels * cols), jnp.float32)
    pieces = []
    for n in range(CHUNKS):
        part, summed = contract(proj, pair_grad, lefts[n], right, summed, n, CHUNKS)
        pieces.append(lax.psum_scatter(part, "col", scatter_dimension=0, tiled=True))
    right_grad = lax.psum_scatter(summed, "row", scatter_dimension=0, tiled=True)
    right_grad = right_grad.reshape(right_own, channels, cols) * (1.0 / sequences)
    left_grad = jnp.concatenate(pieces, axis=1).reshape(own, tile_rows, channels)
    return jnp.transpose(left_grad, (0, 2, 1)), right_grad


def solution(mesh):
    placed = (P("col", None, "row"), P("row", None, "col"), P("row", None, "col"), P())
    return jax.shard_map(
        on_device,
        mesh=mesh,
        in_specs=placed,
        out_specs=(P("col", None, "row"), P("row", None, "col")),
        check_vma=False,
    )
```

profile of v0, /device:TPU:31, one launch (start us, length us, event | category | flops | bytes accessed | tf_op | source)
XLA Modules:
  0.0 540.1 jit_solution(18187773743524983873)
XLA Ops:
  7.2 0.0 copy-start
  7.2 0.0 all-gather.6.cloned.1.call-start
  7.2 0.0 copy-start.1
  7.2 2.0 copy.14
  9.2 2.3 reshape.24
  11.5 0.8 fusion
  12.4 0.0 all-gather.6.cloned.1.call-update
  12.4 0.0 all-gather.8.cloned.1.call-start
  12.4 0.0 copy-done
  12.4 1.1 copy.16
  13.5 0.0 all-gather.8.cloned.1.call-update
  13.5 0.0 all-gather.10.cloned.1.call-start
  13.6 0.7 all-gather.10.cloned.1.call-update
  14.3 0.0 all-gather.12.cloned.1.call-start
  14.3 0.5 all-gather.12.cloned.1.call-update
  14.9 0.0 all-gather.14.cloned.1.call-start
  14.9 0.5 all-gather.14.cloned.1.call-update
  15.5 0.0 reduce-scatter.6.cloned.1.call-start
  15.5 0.0 copy-done.1
  15.5 0.8 copy.13
  16.3 33.3 %all-gather.6.cloned.1.call-done.left_ref = bf16[128,4096]{1,0:T(8,128)(2,1)} async-done(((bf16[16,4096]{1,0:T(8,128)(2,1)}), bf16[128,4096]{1,0:T(8,128)(2,1)}) %all-gather.6.cloned.1.call-update) | async-done | bytes 1048592 | tf_op jit(solution)/shard_map/all_gather | solution.py:93
  49.7 27.0 %all-gather.8.cloned.1.call-done.right_ref = bf16[128,8192]{1,0:T(8,128)(2,1)} async-done(((bf16[32,8192]{1,0:T(8,128)(2,1)}), bf16[128,8192]{1,0:T(8,128)(2,1)}) %all-gather.8.cloned.1.call-update) | async-done | bytes 2097168 | tf_op jit(solution)/shard_map/all_gather | solution.py:88
  76.6 2.4 broadcast_in_dim.3.before_ref
  79.0 83.6 %shard_map.59 = (f32[128,4096]{1,0:T(8,128)}, f32[128,8192]{1,0:T(8,128)}) custom-call(bf16[1024,128]{1,0:T(8,128)(2,1)} %bitcast.17, bf16[512,128,256]{2,1,0:T(8,128)(2,1)} %grad_ref.7, bf16[128,4096]{1,0:T(8,128)(2,1)} %all-gather.6.cloned.1.call-done.left_ref, ...), custom_call_target="tpu_custom_call", output_to_operand_aliasing={{1}: (4, {})} | custom-call | flops 25769803776 | bytes 16777216 | tf_op jit(solution)/shard_map/pallas_call | solution.py:54
  162.6 0.0 reduce-scatter.6.cloned.1.call-update
  162.6 0.0 reduce-scatter.8.cloned.1.call-start
  162.7 0.0 all-gather.10.cloned.1.call-done.left_ref
  162.7 83.6 %shard_map.60 = (f32[128,4096]{1,0:T(8,128)}, f32[128,8192]{1,0:T(8,128)}) custom-call(bf16[1024,128]{1,0:T(8,128)(2,1)} %bitcast.18, bf16[512,128,256]{2,1,0:T(8,128)(2,1)} %grad_ref.7, bf16[128,4096]{1,0:T(8,128)(2,1)} %all-gather.10.cloned.1.call-done.left_ref, ...), custom_call_target="tpu_custom_call", output_to_operand_aliasing={{1}: (4, {})} | custom-call | flops 25769803776 | bytes 16777216 | tf_op jit(solution)/shard_map/pallas_call | solution.py:54
  246.3 0.0 reduce-scatter.8.cloned.1.call-update
  246.4 0.0 reduce-scatter.10.cloned.1.call-start
  246.4 0.0 all-gather.12.cloned.1.call-done.left_ref
  246.4 83.6 %shard_map.61 = (f32[128,4096]{1,0:T(8,128)}, f32[128,8192]{1,0:T(8,128)}) custom-call(bf16[1024,128]{1,0:T(8,128)(2,1)} %bitcast.19, bf16[512,128,256]{2,1,0:T(8,128)(2,1)} %grad_ref.7, bf16[128,4096]{1,0:T(8,128)(2,1)} %all-gather.12.cloned.1.call-done.left_ref, ...), custom_call_target="tpu_custom_call", output_to_operand_aliasing={{1}: (4, {})} | custom-call | flops 25769803776 | bytes 16777216 | tf_op jit(solution)/shard_map/pallas_call | solution.py:54
  330.1 0.0 reduce-scatter.10.cloned.1.call-update
  330.1 0.0 reduce-scatter.12.cloned.1.call-start
  330.2 0.0 all-gather.14.cloned.1.call-done.left_ref
  330.2 83.7 %shard_map.62 = (f32[128,4096]{1,0:T(8,128)}, f32[128,8192]{1,0:T(8,128)}) custom-call(bf16[1024,128]{1,0:T(8,128)(2,1)} %bitcast.20, bf16[512,128,256]{2,1,0:T(8,128)(2,1)} %grad_ref.7, bf16[128,4096]{1,0:T(8,128)(2,1)} %all-gather.14.cloned.1.call-done.left_ref, ...), custom_call_target="tpu_custom_call", output_to_operand_aliasing={{1}: (4, {})} | custom-call | flops 25769803776 | bytes 16777216 | tf_op jit(solution)/shard_map/pallas_call | solution.py:54
  413.9 0.0 reduce-scatter.12.cloned.1.call-update
  413.9 0.0 reduce-scatter.14.cloned.1.call-start
  413.9 0.5 reduce-scatter.14.cloned.1.call-update
  414.5 0.0 reduce-scatter.6.cloned.1.call-done
  414.5 0.0 reduce-scatter.8.cloned.1.call-done
  414.5 0.0 reduce-scatter.10.cloned.1.call-done
  414.6 67.5 %reduce-scatter.12.cloned.1.call-done = f32[16,4096]{1,0:T(8,128)} async-done(((f32[128,4096]{1,0:T(8,128)}), f32[16,4096]{1,0:T(8,128)}) %reduce-scatter.12.cloned.1.call-update) | async-done | bytes 262160 | tf_op jit(solution)/shard_map/reduce_scatter | solution.py:99
  482.0 1.3 pad_maximum_fusion
  483.3 2.8 reshape.26
  486.1 3.6 copy.15
  489.7 41.0 %reduce-scatter.14.cloned.1.call-done = f32[32,8192]{1,0:T(8,128)} async-done(((f32[128,8192]{1,0:T(8,128)}), f32[32,8192]{1,0:T(8,128)}) %reduce-scatter.14.cloned.1.call-update) | async-done | bytes 1048592 | tf_op jit(solution)/shard_map/reduce_scatter | solution.py:100
  530.6 1.3 broadcast_multiply_fusion
  531.9 1.3 copy.17
Async XLA Ops:
  7.2 5.3 copy-start
  7.2 42.5 %all-gather.6.cloned.1.call-start = ((), (), s32[]{:S(2)}) async-start(), calls=%async_computation.5 | async-start | bytes 1179648 | tf_op jit(solution)/shard_map/all_gather | solution.py:93
  7.2 8.3 %copy-start.1 = (bf16[1024,128]{1,0:T(8,128)(2,1)S(1)}, bf16[1024,128]{1,0:T(8,128)(2,1)}, u32[]{:S(2)}) copy-start(bf16[1024,128]{1,0:T(8,128)(2,1)} %param.7) | copy-start | bytes 786436
  12.4 64.3 %all-gather.8.cloned.1.call-start = ((), (), s32[]{:S(2)}) async-start(), calls=%async_computation.6 | async-start | bytes 2621440 | tf_op jit(solution)/shard_map/all_gather | solution.py:88
  13.5 149.2 %all-gather.10.cloned.1.call-start = ((), (), s32[]{:S(2)}) async-start(), calls=%async_computation.8 | async-start | bytes 1179648 | tf_op jit(solution)/shard_map/all_gather | solution.py:93
  14.3 232.2 %all-gather.12.cloned.1.call-start = ((), (), s32[]{:S(2)}) async-start(), calls=%async_computation.10 | async-start | bytes 1179648 | tf_op jit(solution)/shard_map/all_gather | solution.py:93
  14.9 315.3 %all-gather.14.cloned.1.call-start = ((), (), s32[]{:S(2)}) async-start(), calls=%async_computation.12 | async-start | bytes 1179648 | tf_op jit(solution)/shard_map/all_gather | solution.py:93
  15.5 399.0 %reduce-scatter.6.cloned.1.call-start = ((), (), s32[]{:S(2)}) async-start(), calls=%async_computation.7 | async-start | bytes 2359296 | tf_op jit(solution)/shard_map/reduce_scatter | solution.py:99
  162.6 251.9 %reduce-scatter.8.cloned.1.call-start = ((), (), s32[]{:S(2)}) async-start(), calls=%async_computation.9 | async-start | bytes 2359296 | tf_op jit(solution)/shard_map/reduce_scatter | solution.py:99
  246.4 168.2 %reduce-scatter.10.cloned.1.call-start = ((), (), s32[]{:S(2)}) async-start(), calls=%async_computation.11 | async-start | bytes 2359296 | tf_op jit(solution)/shard_map/reduce_scatter | solution.py:99
  330.1 151.9 %reduce-scatter.12.cloned.1.call-start = ((), (), s32[]{:S(2)}) async-start(), calls=%async_computation.13 | async-start | bytes 2359296 | tf_op jit(solution)/shard_map/reduce_scatter | solution.py:99
  413.9 116.8 %reduce-scatter.14.cloned.1.call-start = ((), (), s32[]{:S(2)}) async-start(), calls=%async_computation.14 | async-start | bytes 5242880 | tf_op jit(solution)/shard_map/reduce_scatter | solution.py:100
Sparse Core Ops, SparseCore 0:
  12.5 37.1 all-gather.5
  51.8 24.8 all-gather.7
  78.8 36.6 all-gather.9
  117.4 38.9 all-gather.11
  158.4 39.0 all-gather.13
  200.9 67.6 reduce-scatter.5
  272.2 67.6 reduce-scatter.7
  343.4 67.4 reduce-scatter.9
  414.4 67.6 reduce-scatter.11
  484.4 46.1 reduce-scatter.13
where the time goes:
time: 543 us; the launch traced here: 540 us
  Pallas kernels  335 us (62%)
  waiting for transfers between devices  171 us (31%)
  local copies, waits for them, and re-layouts  17 us (3%)
  between operations  14.3 us (3%)
    pallas_call x4, Pallas kernels, contract(): pl.pallas_call(functools.partial(contract_block, channels, cols, 1.0 / se...  335 us
    reduce_scatter x4, waiting for transfers between devices, on_device(): lax.psum_scatter(part, 'col', scatter_dimension=0, tiled=True)  67.5 us
    reduce_scatter x1, waiting for transfers between devices, on_device(): lax.psum_scatter(summed, 'row', scatter_dimension=0, tiled=True)  41 us
    all_gather x4, waiting for transfers between devices, on_device(): lax.all_gather(left_own[:, n * per:(n + 1) * per], 'col', axis=0, tiled=T...  33.4 us
    all_gather x1, waiting for transfers between devices, on_device(): lax.all_gather(right_factor.reshape(right_own, channels * cols), 'row', a...  27 us
  transfers between devices with their start and end apart: 10, of which 4 were waited for; matrix products, arithmetic and copies ran while one was open for 2% of the time, Pallas kernels for 62%

commit v1 on v0

--- a/solution.py
+++ b/solution.py
@@ -9,6 +9,345 @@
 
 CHUNKS = 4
 BLOCK_ROWS = 16
+PASSES = 2
+FUSED_ROWS = 32
+UNITS = 4
+MESH = pl.DeviceIdType.MESH
+BF16 = jnp.bfloat16
+F32 = jnp.float32
+
+
+def fused_block(
+    n_row, n_col, channels, proj_ref, grad_ref, left_ref, right_ref, out_left_ref, out_right_ref,
+    held_0, held_1, grads, lefts, rights, right_sum, left_sum, left_out, left_in, right_out, right_in, left_done,
+    right_done, grad_sem, own_sem, left_send, left_recv, right_send, right_recv, part_send, part_recv, sum_send, sum_recv,
+):
+    tile_rows, width, cols = grad_ref.shape
+    own, right_own = left_ref.shape[0], right_ref.shape[0]
+    sequences = own * n_col
+    inverse = 1.0 / sequences
+    rows = FUSED_ROWS
+    blocks = tile_rows // rows
+    chunks = blocks // 2
+    pairs = PASSES * chunks
+    some = channels // PASSES
+    high = some * channels
+    wide = some * cols
+    deep = rows * channels
+    span = 2 * deep
+    per_unit = rows // UNITS
+    step = wide // UNITS
+    row, col = lax.axis_index("row"), lax.axis_index("col")
+
+    def to_col(d):
+        return {"col": lax.rem(col + d, n_col)}
+
+    def to_row(d):
+        return {"row": lax.rem(row + d, n_row)}
+
+    def left_copy(d, k):
+        at = pl.ds(pl.multiple_of(k * span, span), span)
+        return pltpu.make_async_remote_copy(
+            left_ref.at[:, at], lefts.at[pl.ds(pl.multiple_of(col * own, own), own), at],
+            left_send.at[d - 1, k], left_recv.at[d - 1, k], device_id=to_col(d), device_id_type=MESH,
+        )
+
+    def right_copy(d, h):
+        at = pl.ds(pl.multiple_of(h * wide, wide), wide)
+        return pltpu.make_async_remote_copy(
+            right_ref.at[:, at], rights.at[pl.ds(pl.multiple_of(row * right_own, right_own), right_own), at],
+            right_send.at[d - 1, h], right_recv.at[d - 1, h], device_id=to_row(d), device_id_type=MESH,
+        )
+
+    def part_copy(d, k):
+        at = pl.ds(pl.multiple_of(k * span, span), span)
+        to = lax.rem(col + d, n_col)
+        return pltpu.make_async_remote_copy(
+            left_out.at[pl.ds(pl.multiple_of(to * own, own), own), at], left_in.at[d - 1, :, at],
+            part_send.at[d - 1, k], part_recv.at[d - 1, k], device_id=to_col(d), device_id_type=MESH,
+        )
+
+    def sum_copy(d, h):
+        at = pl.ds(pl.multiple_of(h * wide, wide), wide)
+        to = lax.rem(row + d, n_row)
+        return pltpu.make_async_remote_copy(
+            right_out.at[pl.ds(pl.multiple_of(to * right_own, right_own), right_own), at], right_in.at[d - 1, :, at],
+            sum_send.at[d - 1, h], sum_recv.at[d - 1, h], device_id=to_row(d), device_id_type=MESH,
+        )
+
+    def grad_copy(t, slot):
+        at = lax.rem(t, blocks) * rows
+        return pltpu.make_async_copy(grad_ref.at[pl.ds(at, rows)], grads.at[slot], grad_sem.at[slot])
+
+    own_left = pltpu.make_async_copy(left_ref, lefts.at[pl.ds(pl.multiple_of(col * own, own), own)], own_sem.at[0])
+    own_right = pltpu.make_async_copy(right_ref, rights.at[pl.ds(pl.multiple_of(row * right_own, right_own), right_own)], own_sem.at[1])
+
+    barrier = pltpu.get_barrier_semaphore()
+
+    @pl.loop(1, n_col)
+    def _(d):
+        pl.semaphore_signal(barrier, inc=1, device_id=to_col(d), device_id_type=MESH)
+
+    @pl.loop(1, n_row)
+    def _(d):
+        pl.semaphore_signal(barrier, inc=1, device_id=to_row(d), device_id_type=MESH)
+
+    grad_copy(0, 0).start()
+    grad_copy(1, 1).start()
+    own_left.start()
+    own_right.start()
+    pl.semaphore_wait(barrier, n_col + n_row - 2)
+
+    @pl.loop(0, PASSES)
+    def _(h):
+        @pl.loop(1, n_row)
+        def _(d):
+            right_copy(d, h).start()
+
+    @pl.loop(0, chunks)
+    def _(k):
+        @pl.loop(1, n_col)
+        def _(d):
+            left_copy(d, k).start()
+
+    right_sum[...] = jnp.zeros_like(right_sum)
+    left_sum[...] = jnp.zeros_like(left_sum)
+
+    def produce(n, h, slot, held):
+        rows_of = pl.ds(pl.multiple_of(h * high, high), high)
+        for r in range(per_unit):
+            i = n * per_unit + r
+            out = jnp.dot(proj_ref[rows_of, :], grads[slot, i], preferred_element_type=F32).astype(BF16)
+            at = pl.ds(pl.multiple_of(i * channels, channels), channels)
+            for e in range(some):
+                held[at, e * cols : (e + 1) * cols] = out[e * channels : (e + 1) * channels]
+
+    def consume(n, h, b, held):
+        inside = pl.ds(pl.multiple_of(n * step, step), step)
+        outside = pl.ds(pl.multiple_of(h * wide + n * step, step), step)
+        deep_at = pl.ds(pl.multiple_of(b * deep, deep), deep)
+        part = held[:, inside]
+        right_sum[:, outside] += jnp.dot(lefts[:, deep_at], part, preferred_element_type=F32)
+        left_sum[deep_at, :] += lax.dot_general(
+            part, rights[:, outside], (((1,), (1,)), ((), ())), preferred_element_type=F32
+        )
+
+    def finish_left(k):
+        piece = min(512, span)
+
+        @pl.loop(0, span // piece)
+        def _(q):
+            at = pl.ds(pl.multiple_of(k * span + q * piece, piece), piece)
+            left_out[:, at] = left_sum[at, :].astype(BF16).T
+
+        return None
+
+    def finish_right(h):
+        piece = min(512, wide)
+
+        @pl.loop(0, wide // piece)
+        def _(q):
+            at = pl.ds(pl.multiple_of(h * wide + q * piece, piece), piece)
+            right_out[:, at] = right_sum[:, at].astype(BF16)
+
+        return None
+
+    def send_left(k):
+        @pl.loop(1, n_col)
+        def _(d):
+            part_copy(d, k).start()
+
+    def send_right(h):
+        @pl.loop(1, n_row)
+        def _(d):
+            sum_copy(d, h).start()
+
+    def total_left(k):
+        @pl.loop(1, n_col)
+        def _(d):
+            part_copy(d, k).wait_recv()
+
+        piece = min(512, span)
+
+        @pl.loop(0, span // piece)
+        def _(q):
+            at = pl.ds(pl.multiple_of(k * span + q * piece, piece), piece)
+            total = left_out[pl.ds(pl.multiple_of(col * own, own), own), at].astype(F32)
+            for d in range(n_col - 1):
+                total += left_in[d, :, at].astype(F32)
+            left_done[:, at] = total * inverse
+
+    def total_right(h):
+        @pl.loop(1, n_row)
+        def _(d):
+            sum_copy(d, h).wait_recv()
+
+        piece = min(512, wide)
+
+        @pl.loop(0, wide // piece)
+        def _(q):
+            at = pl.ds(pl.multiple_of(h * wide + q * piece, piece), piece)
+            total = right_sum[pl.ds(pl.multiple_of(row * right_own, right_own), right_own), at]
+            for d in range(n_row - 1):
+                total += right_in[d, :, at].astype(F32)
+            right_done[:, at] = total * inverse
+
+    def wait_right(h):
+        @pl.loop(1, n_row)
+        def _(d):
+            right_copy(d, h).wait_recv()
+
+    grad_copy(0, 0).wait()
+
+    @pl.loop(0, UNITS)
+    def _(n):
+        produce(n, 0, 0, held_0)
+
+    own_left.wait()
+    own_right.wait()
+    wait_right(0)
+
+    def first_half(p):
+        h, b = p // chunks, lax.rem(p, chunks) * 2
+
+        @pl.when(p < chunks)
+        def _():
+            @pl.loop(1, n_col)
+            def _(d):
+                left_copy(d, p).wait_recv()
+
+        @pl.when(p == chunks)
+        def _():
+            wait_right(1)
+
+        grad_copy(2 * p + 1, 1).wait()
+
+        @pl.when(p < pairs - 1)
+        def _():
+            grad_copy(2 * p + 2, 0).start()
+
+        @pl.loop(0, UNITS)
+        def _(n):
+            produce(n, h, 1, held_1)
+            consume(n, h, b, held_0)
+
+        @pl.when(p == chunks)
+        def _():
+            send_right(0)
+
+        @pl.when(p > chunks)
+        def _():
+            send_left(p - chunks - 1)
+
+    @pl.loop(0, pairs - 1)
+    def _(p):
+        first_half(p)
+        h, b = p // chunks, lax.rem(p, chunks) * 2 + 1
+        ahead = (p + 1) // chunks
+        grad_copy(2 * p + 2, 0).wait()
+        grad_copy(2 * p + 3, 1).start()
+
+        @pl.loop(0, UNITS)
+        def _(n):
+            produce(n, ahead, 0, held_0)
+            consume(n, h, b, held_1)
+
+        @pl.when(p == chunks - 1)
+        def _():
+            finish_right(0)
+
+        @pl.when(p >= chunks)
+        def _():
+            finish_left(p - chunks)
+
+    first_half(pairs - 1)
+
+    @pl.loop(0, UNITS)
+    def _(n):
+        consume(n, PASSES - 1, blocks - 1, held_1)
+
+    finish_right(1)
+    finish_left(chunks - 1)
+    send_right(1)
+    send_left(chunks - 1)
+
+    total_right(0)
+
+    @pl.loop(0, chunks - 1)
+    def _(k):
+        total_left(k)
+
+    total_left(chunks - 1)
+    left_copy_out = pltpu.make_async_copy(left_done, out_left_ref, own_sem.at[0])
+    left_copy_out.start()
+    total_right(1)
+    right_copy_out = pltpu.make_async_copy(right_done, out_right_ref, own_sem.at[1])
+    right_copy_out.start()
+
+    @pl.loop(0, chunks)
+    def _(k):
+        @pl.loop(1, n_col)
+        def _(d):
+            left_copy(d, k).wait_send()
+            part_copy(d, k).wait_send()
+
+    @pl.loop(0, PASSES)
+    def _(h):
+        @pl.loop(1, n_row)
+        def _(d):
+            right_copy(d, h).wait_send()
+            sum_copy(d, h).wait_send()
+
+    left_copy_out.wait()
+    right_copy_out.wait()
+
+
+def fused(proj, grad, left, right, n_row, n_col):
+    tile_rows, width, cols = grad.shape
+    own, right_own = left.shape[0], right.shape[0]
+    channels = left.shape[1] // tile_rows
+    sequences = own * n_col
+    rows = FUSED_ROWS
+    chunks = tile_rows // rows // 2
+    flops = 2 * tile_rows * cols * channels * channels * (width + 2 * sequences)
+    anywhere = pl.BlockSpec(memory_space=pl.ANY)
+    held = pltpu.VMEM((rows * channels, channels // PASSES * cols), BF16)
+    dma = pltpu.SemaphoreType.DMA
+    return pl.pallas_call(
+        functools.partial(fused_block, n_row, n_col, channels),
+        in_specs=[pl.BlockSpec(memory_space=pltpu.VMEM), anywhere, anywhere, anywhere],
+        out_specs=[anywhere, anywhere],
+        out_shape=[jax.ShapeDtypeStruct(left.shape, F32), jax.ShapeDtypeStruct(right.shape, F32)],
+        scratch_shapes=[
+            held,
+            held,
+            pltpu.VMEM((2, rows, width, cols), BF16),
+            pltpu.VMEM((sequences, tile_rows * channels), BF16),
+            pltpu.VMEM((sequences, channels * cols), BF16),
+            pltpu.VMEM((sequences, channels * cols), F32),
+            pltpu.VMEM((tile_rows * channels, sequences), F32),
+            pltpu.VMEM((sequences, tile_rows * channels), BF16),
+            pltpu.VMEM((n_col - 1, own, tile_rows * channels), BF16),
+            pltpu.VMEM((sequences, channels * cols), BF16),
+            pltpu.VMEM((n_row - 1, right_own, channels * cols), BF16),
+            pltpu.VMEM(left.shape, F32),
+            pltpu.VMEM(right.shape, F32),
+            dma((2,)),
+            dma((2,)),
+            dma((n_col - 1, chunks)),
+            dma((n_col - 1, chunks)),
+            dma((n_row - 1, PASSES)),
+            dma((n_row - 1, PASSES)),
+            dma((n_col - 1, chunks)),
+            dma((n_col - 1, chunks)),
+            dma((n_row - 1, PASSES)),
+            dma((n_row - 1, PASSES)),
+        ],
+        compiler_params=pltpu.CompilerParams(
+            collective_id=0, has_side_effects=True, vmem_limit_bytes=62 * 1024 * 1024
+        ),
+        cost_estimate=pl.CostEstimate(flops=flops, bytes_accessed=2 * grad.size * 2, transcendentals=0),
+    )(proj, grad, left, right)
 
 
 def contract_block(channels, cols, inverse, proj_ref, grad_ref, left_ref, right_ref, before_ref, out_left_ref, sum_ref, held):
@@ -80,33 +419,39 @@
     )(proj, grad, left, right, before)
 
 
-def on_device(left_factor, right_factor, pair_grad, projection):
+def gathered(proj, grad, left_own, right_own_flat):
+    sequences_of = functools.partial(lax.all_gather, axis=0, tiled=True)
+    right = sequences_of(right_own_flat, "row")
+    per = left_own.shape[1] // CHUNKS
+    lefts = [sequences_of(left_own[:, n * per : (n + 1) * per], "col") for n in range(CHUNKS)]
+    summed = jnp.zeros(right.shape, jnp.float32)
+    pieces = []
+    for n in range(CHUNKS):
+        part, summed = contract(proj, grad, lefts[n], right, summed, n, CHUNKS)
+        pieces.append(lax.psum_scatter(part, "col", scatter_dimension=0, tiled=True))
+    right_grad = lax.psum_scatter(summed, "row", scatter_dimension=0, tiled=True)
+    return jnp.concatenate(pieces, axis=1), right_grad * (1.0 / right.shape[0])
+
+
+def on_device(n_row, n_col, left_factor, right_factor, pair_grad, projection):
     tile_rows, width, cols = pair_grad.shape
     own, channels, _ = left_factor.shape
     right_own = right_factor.shape[0]
     proj = projection.reshape(channels, channels, width).transpose(1, 0, 2).reshape(channels * channels, width)
-    right = lax.all_gather(right_factor.reshape(right_own, channels * cols), "row", axis=0, tiled=True)
-    sequences = right.shape[0]
-    left_own = jnp.transpose(left_factor, (0, 2, 1)).reshape(own, tile_rows * channels)
-    per = tile_rows * channels // CHUNKS
-    lefts = [
-        lax.all_gather(left_own[:, n * per : (n + 1) * per], "col", axis=0, tiled=True) for n in range(CHUNKS)
-    ]
-    summed = jnp.zeros((sequences, channels * cols), jnp.float32)
-    pieces = []
-    for n in range(CHUNKS):
-        part, summed = contract(proj, pair_grad, lefts[n], right, summed, n, CHUNKS)
-        pieces.append(lax.psum_scatter(part, "col", scatter_dimension=0, tiled=True))
-    right_grad = lax.psum_scatter(summed, "row", scatter_dimension=0, tiled=True)
-    right_grad = right_grad.reshape(right_own, channels, cols) * (1.0 / sequences)
-    left_grad = jnp.concatenate(pieces, axis=1).reshape(own, tile_rows, channels)
-    return jnp.transpose(left_grad, (0, 2, 1)), right_grad
+    right = right_factor.reshape(right_own, channels * cols)
+    left = jnp.transpose(left_factor, (0, 2, 1)).reshape(own, tile_rows * channels)
+    if own % 16 == 0 and right_own % 16 == 0 and cols % 256 == 0 and tile_rows % (4 * FUSED_ROWS) == 0:
+        left_grad, right_grad = fused(proj, pair_grad, left, right, n_row, n_col)
+    else:
+        left_grad, right_grad = gathered(proj, pair_grad, left, right)
+    left_grad = jnp.transpose(left_grad.reshape(own, tile_rows, channels), (0, 2, 1))
+    return left_grad, right_grad.reshape(right_own, channels, cols)
 
 
 def solution(mesh):
     placed = (P("col", None, "row"), P("row", None, "col"), P("row", None, "col"), P())
     return jax.shard_map(
-        on_device,
+        functools.partial(on_device, mesh.shape["row"], mesh.shape["col"]),
         mesh=mesh,
         in_specs=placed,
         out_specs=(P("col", None, "row"), P("row", None, "col")),

time: 543 us -> 289 us (0.53)
  waiting for transfers between devices: 171 us -> 0 us
  Pallas kernels: 335 us -> 270 us
  between operations: 14.3 us -> 0.65 us
    reduce_scatter x5 -> x0, waiting for transfers between devices: 109 us -> none  [the longest x4 67.5 us: on_device(): lax.psum_scatter(part, 'col', scatter_dimension=0, tiled=True)]
    pallas_call x4 -> x1, Pallas kernels: 335 us -> 270 us  [fused(): pl.pallas_call(functools.partial(fused_block, n_row, n_col, channels), in...]
    all_gather x5 -> x0, waiting for transfers between devices: 60.4 us -> none  [the longest x4 33.4 us: on_device(): lax.all_gather(left_own[:, n * per:(n + 1) * per], 'col', axis=0, tiled=T...]
  transfers between devices with their start and end apart: 10 -> 0, of which waited for: 4 -> 0; matrix products, arithmetic and copies ran while one was open for 2% -> 0% of each run, Pallas kernels for 62% -> 0%
where the time goes in v1:
time: 289 us
  Pallas kernels  270 us (93%)
  local copies, waits for them, and re-layouts  18.6 us (6%)
    pallas_call x1, Pallas kernels, fused(): pl.pallas_call(functools.partial(fused_block, n_row, n_col, channels), in...  270 us
    unnamed x3, local copies, waits for them, and re-layouts  8.24 us

profile of v1, /device:TPU:31, one launch (start us, length us, event | category | flops | bytes accessed | tf_op | source)
XLA Modules:
  0.0 288.9 jit_solution(5049353060753378589)
XLA Ops:
  0.6 1.8 copy.9
  2.4 2.1 copy.12
  4.5 1.9 copy.10
  6.5 3.0 %reshape.24.left_ref = bf16[16,16384]{1,0:T(8,128)(2,1)} reshape(bf16[16,512,32]{2,1,0:T(8,128)(2,1)S(1)} %copy.10) | data formatting | bytes 1048576 | tf_op jit(solution)/shard_map/reshape | solution.py:442
  9.4 269.6 %shard_map.59 = (f32[16,16384]{1,0:T(8,128)}, f32[32,8192]{1,0:T(8,128)}) custom-call(bf16[1024,128]{1,0:T(8,128)(2,1)} %bitcast.17, bf16[512,128,256]{2,1,0:T(8,128)(2,1)} %grad_ref.1, bf16[16,16384]{1,0:T(8,128)(2,1)} %reshape.24.left_ref, bf16[32,8192]{1,0:T(8,128)(2,1)} %bitcast.15), custom_call_target="tpu_custom_call" | custom-call | flops 103079215104 | bytes 67108864 | tf_op jit(solution)/shard_map/pallas_call | solution.py:316
  279.1 2.5 copy.13
  281.6 3.7 %reshape.26 = f32[16,512,32]{2,1,0:T(8,128)} reshape(f32[16,16384]{1,0:T(8,128)} %get-tuple-element.4) | data formatting | bytes 2097152 | tf_op jit(solution)/shard_map/reshape | solution.py:447
  285.3 3.6 %copy.11 = f32[16,32,512]{2,1,0:T(8,128)} copy(f32[16,32,512]{1,2,0:T(8,128)} %bitcast.10) | data formatting | bytes 2097152

commit v2 on v1

v2 whole, which is shorter than its diff:
```python
import functools

import jax
import jax.numpy as jnp
from jax import lax
from jax.experimental import pallas as pl
from jax.experimental.pallas import tpu as pltpu
from jax.sharding import PartitionSpec as P

CHUNKS = 4
BLOCK_ROWS = 16
PASSES = 2
FUSED_ROWS = 32
STEP = 1024
AHEAD = 2
LANES = 128
MESH = pl.DeviceIdType.MESH
BF16 = jnp.bfloat16
F32 = jnp.float32


def fused_block(
    n_row, n_col, channels, proj_ref, grad_ref, left_ref, right_ref, out_left_ref, out_right_ref,
    held_0, held_1, proj, proj_wide, left_raw, right_raw, left_final, grads, lefts, rights, right_sum, left_sum, left_out, left_in, right_out, right_in, left_done,
    right_done, grad_sem, out_sem, own_sem, left_send, left_recv, right_send, right_recv, part_send, part_recv, sum_send, sum_recv,
):
    folds, _, width, cols = grad_ref.shape
    tile_rows = folds * LANES
    own, right_own = left_ref.shape[0] // channels, right_ref.shape[0] // channels
    sequences = own * n_col
    inverse = 1.0 / sequences
    rows = FUSED_ROWS
    blocks = tile_rows // rows
    chunks = blocks // 2
    pairs = PASSES * chunks
    some = channels // PASSES
    high = some * channels
    wide = some * cols
    deep = rows * channels
    span = 2 * deep
    step = min(STEP, wide)
    row, col = lax.axis_index("row"), lax.axis_index("col")

    def to_col(d):
        return {"col": lax.rem(col + d, n_col)}

    def to_row(d):
        return {"row": lax.rem(row + d, n_row)}

    half_row, half_col = n_row // 2, n_col // 2
    row_mate = row + 1 - 2 * lax.rem(row, 2)
    col_mate = col + 1 - 2 * lax.rem(col, 2)
    steps = wide // step

    def left_move(n, to, owner, k):
        at = (pl.ds(pl.multiple_of(owner * own, own), own), pl.ds(pl.multiple_of(k * span, span), span))
        return pltpu.make_async_remote_copy(
            lefts.at[at], lefts.at[at], left_send.at[n, k], left_recv.at[n, k], device_id={"col": to}, device_id_type=MESH
        )

    def right_move(n, to, owner, h):
        at = (pl.ds(pl.multiple_of(owner * right_own, right_own), right_own), pl.ds(pl.multiple_of(h * wide, wide), wide))
        return pltpu.make_async_remote_copy(
            rights.at[at], rights.at[at], right_send.at[n, h], right_recv.at[n, h], device_id={"row": to}, device_id_type=MESH
        )

    def give(move, me, mate, half, k):
        for d in range(1, half):
            move(d - 1, lax.rem(me + 2 * d, 2 * half), me, k).start()
        move(half - 1, mate, me, k).start()

    def forward(move, me, mate, half, k):
        for d in range(1, half):
            owner = lax.rem(me + 2 * (half - d), 2 * half)
            move(d - 1, mate, owner, k).wait_recv()
            move(half - 1 + d, mate, owner, k).start()

    def arrive(move, me, mate, half, k):
        for d in range(half):
            owner = lax.rem(mate + 2 * (half - d), 2 * half)
            move(half - 1 + d, mate, owner, k).wait_recv()

    def give_left(k):
        give(left_move, col, col_mate, half_col, k)

    def give_right(h):
        give(right_move, row, row_mate, half_row, h)

    def forward_left(k):
        forward(left_move, col, col_mate, half_col, k)

    def forward_right(h):
        forward(right_move, row, row_mate, half_row, h)

    def arrive_left(k):
        arrive(left_move, col, col_mate, half_col, k)

    def arrive_right(h):
        arrive(right_move, row, row_mate, half_row, h)

    def part_copy(d, k):
        at = pl.ds(pl.multiple_of(k * deep, deep), deep)
        to = lax.rem(col + d, n_col)
        return pltpu.make_async_remote_copy(
            left_out.at[pl.ds(pl.multiple_of(to * own, own), own), at], left_in.at[d - 1, :, at],
            part_send.at[d - 1, k], part_recv.at[d - 1, k], device_id=to_col(d), device_id_type=MESH,
        )

    def sum_copy(d, m):
        at = pl.ds(pl.multiple_of(m * step, step), step)
        to = lax.rem(row + d, n_row)
        return pltpu.make_async_remote_copy(
            right_out.at[pl.ds(pl.multiple_of(to * right_own, right_own), right_own), at], right_in.at[d - 1, :, at],
            sum_send.at[d - 1, m], sum_recv.at[d - 1, m], device_id=to_row(d), device_id_type=MESH,
        )

    def grad_copy(t, slot):
        high_rows = rows // folds
        at = pl.ds(lax.rem(t, blocks) * high_rows, high_rows)
        return pltpu.make_async_copy(grad_ref.at[:, at], grads.at[slot], grad_sem.at[slot])

    own_left = pltpu.make_async_copy(left_ref, left_raw, own_sem.at[0])
    own_right = pltpu.make_async_copy(right_ref, right_raw, own_sem.at[1])
    left_rows = pl.ds(pl.multiple_of(col * own, own), own)
    right_rows = pl.ds(pl.multiple_of(row * right_own, right_own), right_own)

    barrier = pltpu.get_barrier_semaphore()

    @pl.loop(1, n_col)
    def _(d):
        pl.semaphore_signal(barrier, inc=1, device_id=to_col(d), device_id_type=MESH)

    @pl.loop(1, n_row)
    def _(d):
        pl.semaphore_signal(barrier, inc=1, device_id=to_row(d), device_id_type=MESH)

    own_right.start()
    own_left.start()
    grad_copy(0, 0).start()
    grad_copy(1, 1).start()
    own_right.wait()
    halves = cols // LANES
    for u in range(halves):
        right_done[u] = right_raw[:, u * LANES : (u + 1) * LANES].astype(F32)
        for e in range(channels):
            at = e * cols + u * LANES
            rights[right_rows, at : at + LANES] = right_done[u, pl.ds(e, right_own, stride=channels), :].astype(BF16)
    own_left.wait()

    @pl.loop(0, own)
    def _(s):
        at = pl.ds(pl.multiple_of(s * channels, channels), channels)
        square = jnp.concatenate([left_raw[at, r * LANES : (r + 1) * LANES] for r in range(folds)], axis=0)
        left_done[pl.ds(pl.multiple_of(s * LANES, LANES), LANES), :] = square.astype(F32).T

    @pl.loop(0, LANES // 8)
    def _(m):
        for u in range(8):
            q = m * 8 + u
            at = pl.ds(pl.multiple_of(q * LANES, LANES), LANES)
            lefts[left_rows, at] = left_done[pl.ds(q, own, stride=LANES), :].astype(BF16)

    pl.semaphore_wait(barrier, n_col + n_row - 2)

    give_right(0)
    give_left(0)

    proj_wide[...] = proj_ref[...].astype(F32)
    for e in range(channels):
        proj[e * channels : (e + 1) * channels, :] = proj_wide[pl.ds(e, channels, stride=channels), :].astype(BF16)
    right_sum[...] = jnp.zeros_like(right_sum)
    left_sum[...] = jnp.zeros_like(left_sum)

    def produce_rows(first, count, h, slot, held):
        rows_of = pl.ds(pl.multiple_of(h * high, high), high)
        for r in range(count * folds):
            i = first * folds + r
            out = jnp.dot(
                proj[rows_of, :], grads[slot, r % folds, first + r // folds], preferred_element_type=F32
            ).astype(BF16)
            at = pl.ds(pl.multiple_of(i * channels, channels), channels)
            for e in range(some):
                held[at, e * cols : (e + 1) * cols] = out[e * channels : (e + 1) * channels]

    def consume_step(n, h, b, held):
        inside = pl.ds(pl.multiple_of(n * step, step), step)
        outside = pl.ds(pl.multiple_of(h * wide + n * step, step), step)
        deep_at = pl.ds(pl.multiple_of(b * deep, deep), deep)
        part = held[:, inside]
        right_sum[:, outside] += jnp.dot(lefts[:, deep_at], part, preferred_element_type=F32)
        left_sum[deep_at, :] += lax.dot_general(
            part, rights[:, outside], (((1,), (1,)), ((), ())), preferred_element_type=F32
        )

    def both(ahead, slot, into, h, b, held):
        @pl.loop(0, 1)
        def _(n):
            produce_rows(0, rows // folds, ahead, slot, into)
            for q in range(wide // step):
                consume_step(n + q, h, b, held)

    def send_left(k):
        piece = min(512, deep)

        @pl.loop(0, deep // piece)
        def _(q):
            at = pl.ds(pl.multiple_of(k * deep + q * piece, piece), piece)
            left_out[:, at] = left_sum[at, :].astype(BF16).T

        @pl.loop(1, n_col)
        def _(d):
            part_copy(d, k).start()

    def send_right(m):
        at = pl.ds(pl.multiple_of(m * step, step), step)
        right_out[:, at] = right_sum[:, at].astype(BF16)

        @pl.loop(1, n_row)
        def _(d):
            sum_copy(d, m).start()

    def total_left(k):
        @pl.loop(1, n_col)
        def _(d):
            part_copy(d, k).wait_recv()

        piece = min(512, deep)

        @pl.loop(0, deep // piece)
        def _(q):
            at = pl.ds(pl.multiple_of(k * deep + q * piece, piece), piece)
            total = left_out[left_rows, at].astype(F32)
            for d in range(n_col - 1):
                total += left_in[d, :, at].astype(F32)
            total *= inverse
            for u in range(piece // LANES):
                base = (k * deep + q * piece) // LANES + u
                left_done[pl.ds(base, own, stride=LANES), :] = total[:, u * LANES : (u + 1) * LANES]

    def total_right(h):
        @pl.loop(0, steps)
        def _(n):
            @pl.loop(1, n_row)
            def _(d):
                sum_copy(d, h * steps + n).wait_recv()

        @pl.loop(0, some)
        def _(n):
            e = h * some + n
            at = pl.ds(pl.multiple_of(e * cols, cols), cols)
            total = right_sum[right_rows, at]
            for d in range(n_row - 1):
                total += right_in[d, :, at].astype(F32)
            total *= inverse
            for u in range(halves):
                right_done[u, pl.ds(e, right_own, stride=channels), :] = total[:, u * LANES : (u + 1) * LANES]

    grad_copy(0, 0).wait()

    @pl.loop(0, rows // folds)
    def _(n):
        produce_rows(n, 1, 0, 0, held_0)

    forward_left(0)
    forward_right(0)
    give_left(1)
    arrive_right(0)

    def first_half(p):
        h, b = p // chunks, lax.rem(p, chunks) * 2

        @pl.when(p < chunks)
        def _():
            arrive_left(p)

        @pl.when(p < chunks - AHEAD)
        def _():
            give_left(p + AHEAD)

        @pl.when(p == 1)
        def _():
            give_right(1)

        @pl.when(p == 2)
        def _():
            forward_right(1)

        @pl.when(p == chunks)
        def _():
            arrive_right(1)

        grad_copy(2 * p + 1, 1).wait()

        @pl.when(p < pairs - 1)
        def _():
            grad_copy(2 * p + 2, 0).start()

        both(h, 1, held_1, h, b, held_0)

        @pl.when(p < chunks - 1)
        def _():
            forward_left(p + 1)

        @pl.when(p >= chunks)
        def _():
            send_left(b)

    @pl.loop(0, pairs - 1)
    def _(p):
        first_half(p)
        h, b = p // chunks, lax.rem(p, chunks) * 2 + 1
        ahead = (p + 1) // chunks
        grad_copy(2 * p + 2, 0).wait()
        grad_copy(2 * p + 3, 1).start()

        both(ahead, 0, held_0, h, b, held_1)

        @pl.when(p == chunks - 1)
        def _():
            @pl.loop(0, steps)
            def _(n):
                send_right(n)

        @pl.when(p >= chunks)
        def _():
            send_left(b)

    first_half(pairs - 1)

    @pl.loop(0, steps)
    def _(n):
        consume_step(n, PASSES - 1, blocks - 1, held_1)
        send_right((PASSES - 1) * steps + n)

    send_left(blocks - 1)
    total_right(0)

    @pl.loop(0, blocks)
    def _(k):
        total_left(k)

    @pl.loop(0, own)
    def _(s):
        square = left_done[pl.ds(pl.multiple_of(s * LANES, LANES), LANES), :].T
        at = pl.ds(pl.multiple_of(s * channels, channels), channels)
        for r in range(folds):
            left_final[at, r * LANES : (r + 1) * LANES] = square[r * channels : (r + 1) * channels]

    left_copy_out = pltpu.make_async_copy(left_final, out_left_ref, own_sem.at[0])
    left_copy_out.start()
    total_right(1)
    right_copies_out = [
        pltpu.make_async_copy(right_done.at[u], out_right_ref.at[:, u * LANES : (u + 1) * LANES], out_sem.at[u])
        for u in range(halves)
    ]
    for copy in right_copies_out:
        copy.start()

    @pl.loop(0, chunks)
    def _(k):
        @pl.loop(0, n_col - 1)
        def _(n):
            left_move(n, col_mate, col, k).wait_send()

    @pl.loop(0, blocks)
    def _(k):
        @pl.loop(1, n_col)
        def _(d):
            part_copy(d, k).wait_send()

    @pl.loop(0, PASSES)
    def _(h):
        @pl.loop(0, n_row - 1)
        def _(n):
            right_move(n, row_mate, row, h).wait_send()

    @pl.loop(0, PASSES * steps)
    def _(m):
        @pl.loop(1, n_row)
        def _(d):
            sum_copy(d, m).wait_send()

    left_copy_out.wait()
    for copy in right_copies_out:
        copy.wait()


def fused(proj, grad, left, right, n_row, n_col):
    tile_rows, width, cols = grad.shape
    own, channels, _ = left.shape
    right_own = right.shape[0]
    folds = tile_rows // LANES
    grad = grad.reshape(folds, LANES, width, cols)
    left = left.reshape(own * channels, tile_rows)
    right = right.reshape(right_own * channels, cols)
    sequences = own * n_col
    rows = FUSED_ROWS
    chunks = tile_rows // rows // 2
    wide = channels // PASSES * cols
    steps = wide // min(STEP, wide)
    flops = 2 * tile_rows * cols * channels * channels * (width + 2 * sequences)
    anywhere = pl.BlockSpec(memory_space=pl.ANY)
    held = pltpu.VMEM((rows * channels, channels // PASSES * cols), BF16)
    dma = pltpu.SemaphoreType.DMA
    return pl.pallas_call(
        functools.partial(fused_block, n_row, n_col, channels),
        in_specs=[pl.BlockSpec(memory_space=pltpu.VMEM), anywhere, anywhere, anywhere],
        out_specs=[anywhere, anywhere],
        out_shape=[jax.ShapeDtypeStruct(left.shape, F32), jax.ShapeDtypeStruct(right.shape, F32)],
        scratch_shapes=[
            held,
            held,
            pltpu.VMEM(proj.shape, BF16),
            pltpu.VMEM(proj.shape, F32),
            pltpu.VMEM(left.shape, BF16),
            pltpu.VMEM(right.shape, BF16),
            pltpu.VMEM(left.shape, F32),
            pltpu.VMEM((2, folds, rows // folds, width, cols), BF16),
            pltpu.VMEM((sequences, tile_rows * channels), BF16),
            pltpu.VMEM((sequences, channels * cols), BF16),
            pltpu.VMEM((sequences, channels * cols), F32),
            pltpu.VMEM((tile_rows * channels, sequences), F32),
            pltpu.VMEM((sequences, tile_rows * channels), BF16),
            pltpu.VMEM((n_col - 1, own, tile_rows * channels), BF16),
            pltpu.VMEM((sequences, channels * cols), BF16),
            pltpu.VMEM((n_row - 1, right_own, channels * cols), BF16),
            pltpu.VMEM((own * LANES, folds * channels), F32),
            pltpu.VMEM((cols // LANES, right_own * channels, LANES), F32),
            dma((2,)),
            dma((cols // LANES,)),
            dma((2,)),
            dma((n_col - 1, chunks)),
            dma((n_col - 1, chunks)),
            dma((n_row - 1, PASSES)),
            dma((n_row - 1, PASSES)),
            dma((n_col - 1, 2 * chunks)),
            dma((n_col - 1, 2 * chunks)),
            dma((n_row - 1, PASSES * steps)),
            dma((n_row - 1, PASSES * steps)),
        ],
        compiler_params=pltpu.CompilerParams(
            collective_id=0, has_side_effects=True, vmem_limit_bytes=62 * 1024 * 1024
        ),
        cost_estimate=pl.CostEstimate(flops=flops, bytes_accessed=2 * grad.size * 2, transcendentals=0),
    )(proj, grad, left, right)


def contract_block(channels, cols, inverse, proj_ref, grad_ref, left_ref, right_ref, before_ref, out_left_ref, sum_ref, held):
    rows = grad_ref.shape[0]

    @pl.when(pl.program_id(0) == 0)
    def _():
        sum_ref[...] = before_ref[...]

    @pl.loop(0, rows)
    def _(i):
        wide = jnp.dot(proj_ref[...], grad_ref[i], preferred_element_type=jnp.float32)
        wide = wide.astype(jnp.bfloat16)
        at = pl.ds(pl.multiple_of(i * channels, channels), channels)
        for e in range(channels):
            held[at, e * cols : (e + 1) * cols] = wide[e * channels : (e + 1) * channels]

    total = channels * cols
    step = min(1024, total)
    out_left_ref[...] = jnp.zeros_like(out_left_ref)

    @pl.loop(0, total // step)
    def _(n):
        at = pl.ds(pl.multiple_of(n * step, step), step)
        part = held[:, at]
        sum_ref[:, at] += jnp.dot(left_ref[...], part, preferred_element_type=jnp.float32)
        out_left_ref[...] += lax.dot_general(
            right_ref[:, at], part, (((1,), (1,)), ((), ())), preferred_element_type=jnp.float32
        )

    out_left_ref[...] *= inverse


def contract(proj, grad, left, right, before, chunk, chunks):
    tile_rows, width, cols = grad.shape
    sequences = left.shape[0]
    rows = tile_rows // chunks
    channels = left.shape[1] // rows
    block = min(BLOCK_ROWS, rows)
    steps = rows // block
    flops = 2 * rows * cols * channels * channels * (width + 2 * sequences)
    whole = lambda shape: pl.BlockSpec(shape, lambda n: (0, 0))
    return pl.pallas_call(
        functools.partial(contract_block, channels, cols, 1.0 / sequences),
        grid=(steps,),
        in_specs=[
            whole(proj.shape),
            pl.BlockSpec((block, width, cols), lambda n: (chunk * steps + n, 0, 0)),
            pl.BlockSpec((sequences, block * channels), lambda n: (0, n)),
            whole(right.shape),
            whole(before.shape),
        ],
        out_specs=[
            pl.BlockSpec((sequences, block * channels), lambda n: (0, n)),
            whole(before.shape),
        ],
        out_shape=[
            jax.ShapeDtypeStruct((sequences, rows * channels), jnp.float32),
            jax.ShapeDtypeStruct(before.shape, jnp.float32),
        ],
        scratch_shapes=[pltpu.VMEM((block * channels, channels * cols), jnp.bfloat16)],
        input_output_aliases={4: 1},
        compiler_params=pltpu.CompilerParams(
            dimension_semantics=("arbitrary",), vmem_limit_bytes=56 * 1024 * 1024
        ),
        cost_estimate=pl.CostEstimate(
            flops=flops, bytes_accessed=rows * width * cols * 2 + before.size * 8, transcendentals=0
        ),
    )(proj, grad, left, right, before)


def gathered(proj, grad, left_own, right_own_flat):
    sequences_of = functools.partial(lax.all_gather, axis=0, tiled=True)
    right = sequences_of(right_own_flat, "row")
    per = left_own.shape[1] // CHUNKS
    lefts = [sequences_of(left_own[:, n * per : (n + 1) * per], "col") for n in range(CHUNKS)]
    summed = jnp.zeros(right.shape, jnp.float32)
    pieces = []
    for n in range(CHUNKS):
        part, summed = contract(proj, grad, lefts[n], right, summed, n, CHUNKS)
        pieces.append(lax.psum_scatter(part, "col", scatter_dimension=0, tiled=True))
    right_grad = lax.psum_scatter(summed, "row", scatter_dimension=0, tiled=True)
    return jnp.concatenate(pieces, axis=1), right_grad * (1.0 / right.shape[0])


def on_device(n_row, n_col, left_factor, right_factor, pair_grad, projection):
    tile_rows, width, cols = pair_grad.shape
    own, channels, _ = left_factor.shape
    right_own = right_factor.shape[0]
    folds = tile_rows // LANES
    fits = own % 16 == 0 and right_own % 16 == 0 and cols % 256 == 0 and tile_rows % LANES == 0
    fits = fits and n_row % 2 == 0 and n_col % 2 == 0 and tile_rows // FUSED_ROWS >= 8
    if fits and folds * channels == LANES and FUSED_ROWS % folds == 0:
        left_grad, right_grad = fused(projection, pair_grad, left_factor, right_factor, n_row, n_col)
        return left_grad.reshape(left_factor.shape), right_grad.reshape(right_factor.shape)
    proj = projection.reshape(channels, channels, width).transpose(1, 0, 2).reshape(channels * channels, width)
    right = right_factor.reshape(right_own, channels * cols)
    left = jnp.transpose(left_factor, (0, 2, 1)).reshape(own, tile_rows * channels)
    left_grad, right_grad = gathered(proj, pair_grad, left, right)
    left_grad = jnp.transpose(left_grad.reshape(own, tile_rows, channels), (0, 2, 1))
    return left_grad, right_grad.reshape(right_own, channels, cols)


def solution(mesh):
    placed = (P("col", None, "row"), P("row", None, "col"), P("row", None, "col"), P())
    return jax.shard_map(
        functools.partial(on_device, mesh.shape["row"], mesh.shape["col"]),
        mesh=mesh,
        in_specs=placed,
        out_specs=(P("col", None, "row"), P("row", None, "col")),
        check_vma=False,
    )
```

time: 289 us -> 223 us (0.77)
  Pallas kernels: 270 us -> 216 us
  local copies, waits for them, and re-layouts: 18.6 us -> 4.6 us
    pallas_call x1, Pallas kernels: 270 us -> 216 us  [fused(): pl.pallas_call(functools.partial(fused_block, n_row, n_col, channels), in...]
    reshape x3 -> x0, local copies, waits for them, and re-layouts: 8.47 us -> none  [the longest x1 3.74 us: on_device(): left_grad.reshape(own, tile_rows, channels)]
    unnamed x3 -> x2, local copies, waits for them, and re-layouts: 8.24 us -> 4.6 us
where the time goes in v2:
time: 223 us; the launch traced here: 222 us
  Pallas kernels  216 us (97%)
  local copies, waits for them, and re-layouts  4.6 us (2%)
    pallas_call x1, Pallas kernels, fused(): pl.pallas_call(functools.partial(fused_block, n_row, n_col, channels), in...  216 us
    unnamed x2, local copies, waits for them, and re-layouts  4.6 us

profile of v2, /device:TPU:31, one launch (start us, length us, event | category | flops | bytes accessed | tf_op | source)
XLA Modules:
  0.0 221.6 jit_solution(14353821967655445693)
XLA Ops:
  0.6 216.4 %shard_map.59 = (f32[512,512]{1,0:T(8,128)}, f32[1024,256]{1,0:T(8,128)}) custom-call(bf16[1024,128]{1,0:T(8,128)(2,1)} %proj_ref.1, bf16[4,128,128,256]{3,2,1,0:T(8,128)(2,1)} %bitcast.7, bf16[512,512]{1,0:T(8,128)(2,1)} %bitcast.8, bf16[1024,256]{1,0:T(8,128)(2,1)} %bitcast.9), custom_call_target="tpu_custom_call" | custom-call | flops 103079215104 | bytes 67108864 | tf_op jit(solution)/shard_map/pallas_call | solution.py:405
  217.0 2.3 %copy.8 = f32[16,32,512]{2,1,0:T(8,128)} copy(f32[16,32,512]{2,1,0:T(8,128)} %bitcast.6) | data formatting | bytes 2097152
  219.3 2.3 %copy.9 = f32[32,32,256]{2,1,0:T(8,128)} copy(f32[32,32,256]{2,1,0:T(8,128)} %bitcast.5) | data formatting | bytes 2097152
